TPU v7x, 1024 devices: a whole 4x8x16 slice. The times are simulated.
1024 devices in a mesh: outer: 64 (over z, y_lo, core), inner: 16 (over y_hi, x).
Axes of the slice: x: 4, y: 8 (y_hi: 4, y_lo: 2; y = y_hi * 2 + y_lo), z: 16, core: 2. Of those that a mesh axis runs over, the one named last changes fastest.
Arguments:
- tokens: bfloat16 [131072, 12288], P(('outer', 'inner')), may hold values from -16 to 16
- cotangent: bfloat16 [131072, 128], P(('outer', 'inner')), may hold values from -8 to 8
- secondary: bfloat16 [12288, 128], P('inner'), may hold values from -0.0546875 to 0.0546875
- master: float32 [12288, 128], P(('inner', 'outer')), may hold values from -6 to 6
- m_code: bfloat16 [12288, 128], P(('inner', 'outer')), may hold values from -1 to 1
- v_code: bfloat16 [12288, 128], P(('inner', 'outer')), may hold values from 0.049804688 to 1
- m_scale: float32 [3072], P(('inner', 'outer')), may hold values from 0.02 to 0.2
- v_scale: float32 [3072], P(('inner', 'outer')), may hold values from 0.001 to 0.02
Outputs:
- projected: bfloat16 [131072, 128], P(('outer', 'inner'))
- master_new: float32 [12288, 128], P(('inner', 'outer'))
- m_code_new: bfloat16 [12288, 128], P(('inner', 'outer'))
- v_code_new: bfloat16 [12288, 128], P(('inner', 'outer'))
- m_scale_new: float32 [3072], P(('inner', 'outer'))
- v_scale_new: float32 [3072], P(('inner', 'outer'))
- secondary_new: bfloat16 [12288, 128], P('inner')
All inputs are finite; a program needn't handle non-finite values. Where the computation divides by a largest or mean magnitude, that divisor is 1e-20 or more.
Results may differ from a plain program's by a relative error of at most 0.009.
Values may be sent and summed in bfloat16 or wider, within the bound.
No kernel may reach another device: no remote copies, remote signals or barrier semaphores. Data moves between devices by JAX's collectives and lax.ppermute only.
A program may use at most 32 MiB of HBM per device.

v0:
```python
import functools
import math

import jax
import jax.numpy as jnp
from jax import lax
from jax.sharding import Mesh
from jax.sharding import PartitionSpec as P

INNER = ("inner_0", "inner_1")
OUTER = ("outer_0", "outer_1", "outer_2")
OUTER_INNER = ("outer_0", "outer_1", "outer_2", "inner_0", "inner_1")
INNER_OUTER = ("inner_0", "inner_1", "outer_0", "outer_1", "outer_2")


def in_blocks(value, dim, devices):
    dims = value.shape
    pieces = value.reshape(*dims[:dim], devices, dims[dim] // devices, *dims[dim + 1 :])
    return jnp.moveaxis(pieces, dim, 0)


def summed_on_arrival(value, axis, dim):
    devices = lax.axis_size(axis)
    pieces = lax.all_to_all(in_blocks(value, dim, devices), axis, 0, 0, tiled=True)
    return jnp.sum(pieces, axis=0)


def by_axis(value, axes):
    return functools.reduce(lax.psum, axes, value)


def joined_along(pieces, dim):
    dims = list(pieces.shape[1:])
    dims[dim] *= pieces.shape[0]
    return jnp.moveaxis(pieces, 0, dim).reshape(dims)


def sent_to_all(value, axis):
    copies = jnp.broadcast_to(value, (lax.axis_size(axis), *value.shape))
    return lax.all_to_all(copies, axis, split_axis=0, concat_axis=0, tiled=True)


def collect(value, axis, dim):
    return joined_along(sent_to_all(value, axis), dim)


def adam_update(gradient, factor, master, m_code, v_code, m_scale, v_scale):
    blocks = m_scale.shape[0]
    height = master.shape[0] // blocks
    shaped = (blocks, height, master.shape[1])
    m_old = (m_code.astype(jnp.float32).reshape(shaped) * m_scale[:, None, None]).reshape(
        master.shape
    )
    v_old = (v_code.astype(jnp.float32).reshape(shaped) * v_scale[:, None, None]).reshape(
        master.shape
    )
    scaled = factor * gradient
    moment = 0.9 * m_old + 0.1 * scaled
    second = 0.95 * v_old + 0.05 * scaled * scaled
    master_new = master - 0.01 * (moment / (jnp.sqrt(second) + 1e-08) + 0.1 * master)
    moment_blocks = moment.reshape(blocks, -1)
    second_blocks = second.reshape(blocks, -1)
    m_scale_new = jnp.max(jnp.abs(moment_blocks), axis=1) + 1e-06
    v_scale_new = jnp.max(second_blocks, axis=1) + 1e-06
    m_code_new = (moment_blocks / m_scale_new[:, None]).reshape(master.shape).astype(jnp.bfloat16)
    v_code_new = (second_blocks / v_scale_new[:, None]).reshape(master.shape).astype(jnp.bfloat16)
    return (master_new, m_code_new, v_code_new, m_scale_new, v_scale_new)


def rounded_term(columns, cotangent):
    part = lax.dot_general(
        columns, cotangent, (((0,), (0,)), ((), ())), preferred_element_type=jnp.float32
    )
    part = lax.optimization_barrier(part.astype(jnp.bfloat16))
    return part.astype(jnp.float32)


def body(tokens, cotangent, secondary, master, m_code, v_code, m_scale, v_scale):
    width = tokens.shape[1]
    columns = tokens
    projected = jnp.dot(
        columns,
        lax.all_gather(secondary, INNER, axis=0, tiled=True),
        preferred_element_type=jnp.float32,
    ).astype(jnp.bfloat16)
    columns = tokens
    group_rows = lax.psum_scatter(
        rounded_term(columns, cotangent).astype(jnp.bfloat16),
        INNER,
        scatter_dimension=0,
        tiled=True,
    ).astype(jnp.float32)
    gradient = summed_on_arrival(group_rows, OUTER, 0)
    total = by_axis(jnp.sum(gradient * gradient), OUTER_INNER)
    limit = 0.25 * math.sqrt(width * secondary.shape[1])
    factor = limit / jnp.maximum(jnp.sqrt(total), limit)
    master_new, m_code_new, v_code_new, m_scale_new, v_scale_new = adam_update(
        gradient, factor, master, m_code, v_code, m_scale, v_scale
    )
    secondary_new = collect(master_new.astype(jnp.bfloat16), OUTER, 0)
    return (projected, master_new, m_code_new, v_code_new, m_scale_new, v_scale_new, secondary_new)


def solution(mesh):
    split = Mesh(
        mesh.devices.reshape(16, 2, 2, 4, 4),
        ("outer_0", "outer_1", "outer_2", "inner_0", "inner_1"),
    )
    return jax.shard_map(
        body,
        mesh=split,
        in_specs=(
            P(OUTER_INNER, None),
            P(OUTER_INNER, None),
            P(INNER, None),
            P(INNER_OUTER, None),
            P(INNER_OUTER, None),
            P(INNER_OUTER, None),
            P(INNER_OUTER),
            P(INNER_OUTER),
        ),
        out_specs=(
            P(OUTER_INNER, None),
            P(INNER_OUTER, None),
            P(INNER_OUTER, None),
            P(INNER_OUTER, None),
            P(INNER_OUTER),
            P(INNER_OUTER),
            P(INNER, None),
        ),
        check_vma=False,
    )
```

profile of v0, /device:TPU:1, one launch (start us, length us, event | category | flops | bytes accessed | tf_op | source)
XLA Modules:
  0.0 281.7 jit_solution(15734408875335111786)
XLA Ops:
  7.2 1.8 copy-done
  9.1 3.5 %convolution_convert_fusion = bf16[12288,128]{1,0:T(8,128)(2,1)} fusion(bf16[128,12288]{1,0:T(8,128)(2,1)S(1)} %copy-done, bf16[128,128]{1,0:T(8,128)(2,1)} %param.9), kind=kOutput, calls=%fused_computation | convolution fusion | flops 404226048 | bytes 6324224 | tf_op jit(solution)/shard_map/dot_general | solution.py:71
  12.6 0.7 all-gather.2.cloned.1.call-update
  13.3 115.0 %reduce-scatter.2.cloned.1.call-done = bf16[768,128]{1,0:T(8,128)(2,1)} async-done(((bf16[12288,128]{1,0:T(8,128)(2,1)}), bf16[768,128]{1,0:T(8,128)(2,1)}) %reduce-scatter.2.cloned.1.call-update) | async-done | bytes 196624 | tf_op jit(solution)/shard_map/reduce_scatter | solution.py:87
  128.4 1.8 reshape.49
  130.1 49.1 %all_to_all.10 = f32[64,12,128]{2,1,0:T(8,128)} all-to-all(f32[64,12,128]{2,1,0:T(8,128)} %reshape.49), channel_id=1, replica_groups=mesh['outer_0'=16,'outer_1'=2,'outer_2'=2,'inner_0'=4,'inner_1'=4] {'out..., dimensions={0} | all-to-all | bytes 786432 | tf_op jit(solution)/shard_map/all_to_all | solution.py:24
  179.2 1.1 reduce_sum.18
  180.3 0.6 multiply_reduce_fusion
  180.9 22.8 %psum.35 = f32[]{:T(128)} all-reduce(f32[]{:T(128)} %multiply_reduce_fusion), channel_id=1, replica_groups=mesh['outer_0'=16,'outer_1'=2,'outer_2'=2,'inner_0'=4,'inner_1'=4] {'out..., use_global_device_ids=true, to_apply=%region_3.0 | all-reduce | flops 1 | bytes 8 | tf_op jit(solution)/shard_map/psum | solution.py:29
  203.7 4.9 %psum.36 = f32[]{:T(128)} all-reduce(f32[]{:T(128)} %psum.35), channel_id=1, replica_groups=mesh['outer_0'=16,'outer_1'=2,'outer_2'=2,'inner_0'=4,'inner_1'=4] {'out..., use_global_device_ids=true, to_apply=%region_4.0 | all-reduce | flops 1 | bytes 8 | tf_op jit(solution)/shard_map/psum | solution.py:29
  208.7 10.6 %psum.37 = f32[]{:T(128)} all-reduce(f32[]{:T(128)} %psum.36), channel_id=1, replica_groups=mesh['outer_0'=16,'outer_1'=2,'outer_2'=2,'inner_0'=4,'inner_1'=4] {'out..., use_global_device_ids=true, to_apply=%region_5.0 | all-reduce | flops 1 | bytes 8 | tf_op jit(solution)/shard_map/psum | solution.py:29
  219.4 0.1 mul.79
  219.5 8.6 %psum.38 = f32[]{:T(128)} all-reduce(f32[]{:T(128)} %psum.37), channel_id=1, replica_groups=mesh['outer_0'=16,'outer_1'=2,'outer_2'=2,'inner_0'=4,'inner_1'=4] {'inn..., use_global_device_ids=true, to_apply=%region_6.0 | all-reduce | flops 1 | bytes 8 | tf_op jit(solution)/shard_map/psum | solution.py:29
  228.2 0.1 mul.69
  228.2 9.1 %psum.39 = f32[]{:T(128)} all-reduce(f32[]{:T(128)} %psum.38), channel_id=1, replica_groups=mesh['outer_0'=16,'outer_1'=2,'outer_2'=2,'inner_0'=4,'inner_1'=4] {'inn..., use_global_device_ids=true, to_apply=%region_7.0 | all-reduce | flops 1 | bytes 8 | tf_op jit(solution)/shard_map/psum | solution.py:29
  238.1 0.8 fusion.1
  238.9 0.8 broadcast_in_dim.2
  239.7 12.2 %all-to-all-start.1 = ((bf16[64,12,128]{2,1,0:T(8,128)(2,1)}), bf16[64,12,128]{2,1,0:T(8,128)(2,1)S(1)}, u32[]{:S(2)}, u32[]{:S(2)}) async-start(bf16[64,12,128]{2,1,0:T(8,128)(2,1)} %broadcast_in_dim.2), calls=%async_computation.2 | async-start | bytes 524288 | tf_op jit(solution)/shard_map/all_to_all | solution.py:40
  251.9 3.5 %convolution_convert_fusion.1 = bf16[128,128]{1,0:T(8,128)(2,1)} fusion(bf16[128,12288]{1,0:T(8,128)(2,1)S(1)} %copy-done, bf16[12288,128]{1,0:T(8,128)(2,1)} %all-gather.2.cloned.1.call-done), kind=kOutput, calls=%fused_computation.1 | convolution fusion | flops 402669568 | bytes 6324224 | tf_op jit(solution)/shard_map/dot_general | solution.py:81
  255.5 0.1 reduce_max.37
  255.6 0.1 reduce_max.25
  256.1 0.7 divide_convert_fusion
  256.8 17.3 %all-to-all-done.1 = bf16[64,12,128]{2,1,0:T(8,128)(2,1)S(1)} async-done(((bf16[64,12,128]{2,1,0:T(8,128)(2,1)}), bf16[64,12,128]{2,1,0:T(8,128)(2,1)S(1)}, u32[]{:S(2)}, u32[]{:S(2)}) %all-to-all-start.1) | async-done | bytes 196640 | tf_op jit(solution)/shard_map/all_to_all | solution.py:40
  274.1 0.7 reshape.47
  (28 shorter events, 0.8 us)
Async XLA Ops:
  7.2 1.9 copy-start
  7.2 121.2 %reduce-scatter.2.cloned.1.call-start = ((), (), s32[]{:S(2)}) async-start(), calls=%async_computation.4 | async-start | bytes 3342336 | tf_op jit(solution)/shard_map/reduce_scatter | solution.py:87
  12.5 206.8 %copy-start.6 = (f32[3]{0:T(128)S(1)}, f32[3]{0:T(128)}, u32[]{:S(2)}) copy-start(f32[3]{0:T(128)} %param.15) | copy-start | bytes 40
  12.6 215.5 %copy-start.7 = (f32[3]{0:T(128)S(1)}, f32[3]{0:T(128)}, u32[]{:S(2)}) copy-start(f32[3]{0:T(128)} %param.14) | copy-start | bytes 40
  12.6 225.5 %copy-start.1 = (bf16[12,128]{1,0:T(8,128)(2,1)S(1)}, bf16[12,128]{1,0:T(8,128)(2,1)}, u32[]{:S(2)}) copy-start(bf16[12,128]{1,0:T(8,128)(2,1)} %param.13) | copy-start | bytes 9220
  12.6 225.5 %copy-start.2 = (bf16[12,128]{1,0:T(8,128)(2,1)S(1)}, bf16[12,128]{1,0:T(8,128)(2,1)}, u32[]{:S(2)}) copy-start(bf16[12,128]{1,0:T(8,128)(2,1)} %param.12) | copy-start | bytes 9220
  12.6 225.5 %copy-start.3 = (f32[12,128]{1,0:T(8,128)S(1)}, f32[12,128]{1,0:T(8,128)}, u32[]{:S(2)}) copy-start(f32[12,128]{1,0:T(8,128)} %param.11) | copy-start | bytes 18436
  12.6 239.3 %all-gather.2.cloned.1.call-start = ((), (), s32[]{:S(2)}) async-start(), calls=%async_computation.3 | async-start | bytes 3342336 | tf_op jit(solution)/shard_map/all_gather | solution.py:83
  239.7 34.5 %all-to-all-start.1 = ((bf16[64,12,128]{2,1,0:T(8,128)(2,1)}), bf16[64,12,128]{2,1,0:T(8,128)(2,1)S(1)}, u32[]{:S(2)}, u32[]{:S(2)}) async-start(bf16[64,12,128]{2,1,0:T(8,128)(2,1)} %broadcast_in_dim.2), calls=%async_computation.2 | async-start | bytes 524288 | tf_op jit(solution)/shard_map/all_to_all | solution.py:40
  255.8 19.1 %copy-start.4 = (f32[3]{0:T(128)}, f32[3]{0:T(128)S(1)}, u32[]{:S(2)}) copy-start(f32[3]{0:T(128)S(1)} %get-tuple-element.15) | copy-start | bytes 40
  255.8 19.1 %copy-start.5 = (f32[3]{0:T(128)}, f32[3]{0:T(128)S(1)}, u32[]{:S(2)}) copy-start(f32[3]{0:T(128)S(1)} %get-tuple-element.16) | copy-start | bytes 40
Sparse Core Ops, SparseCore 0:
  13.4 114.9 reduce-scatter.1
  132.6 83.7 all-gather.1
where the time goes:
time: 282 us
  waiting for transfers between devices  133 us (47%)
  blocking collectives  105 us (37%)
  between operations  14.9 us (5%)
  starting transfers between devices  12.3 us (4%)
  matrix products  6.96 us (2%)
  local copies, waits for them, and re-layouts  5.89 us (2%)
  other arithmetic  3.44 us (1%)
    reduce_scatter x1, waiting for transfers between devices, body(): lax.psum_scatter(rounded_term(columns, cotangent).astype(jnp.bfloat16), I...  115 us
    psum x5, blocking collectives, by_axis(): return functools.reduce(lax.psum, axes, value)  56.1 us
    all_to_all x1, blocking collectives, summed_on_arrival(): lax.all_to_all(in_blocks(value, dim, devices), axis, 0, 0, tiled=True)  49.1 us
    all_to_all x1, waiting for transfers between devices, sent_to_all(): return lax.all_to_all(copies, axis, split_axis=0, concat_axis=0, tiled=True)  17.3 us
    all_to_all x1, starting transfers between devices, sent_to_all(): return lax.all_to_all(copies, axis, split_axis=0, concat_axis=0, tiled=True)  12.2 us
  transfers between devices with their start and end apart: 3, of which 2 were waited for; matrix products, arithmetic and copies ran while one was open for 4% of the time, Pallas kernels for 0%

commit v1 on v0

v1 whole, which is shorter than its diff:
```python
import math

import jax
import jax.numpy as jnp
from jax import lax
from jax.sharding import Mesh
from jax.sharding import PartitionSpec as P

INNER = ("yh", "x")
OUTER = ("z", "yl", "c")
OUTER_INNER = OUTER + INNER
INNER_OUTER = INNER + OUTER
bf16, f32 = jnp.bfloat16, jnp.float32


def exchange(pieces, axes):
    return lax.all_to_all(pieces, axes, split_axis=0, concat_axis=0, tiled=True)


def to_all(value, axes):
    return exchange(jnp.broadcast_to(value, (lax.axis_size(axes), *value.shape)), axes)


def adam_update(gradient, factor, master, m_code, v_code, m_scale, v_scale):
    blocks = m_scale.shape[0]
    height = master.shape[0] // blocks
    shaped = (blocks, height, master.shape[1])
    m_old = (m_code.astype(f32).reshape(shaped) * m_scale[:, None, None]).reshape(master.shape)
    v_old = (v_code.astype(f32).reshape(shaped) * v_scale[:, None, None]).reshape(master.shape)
    scaled = factor * gradient
    moment = 0.9 * m_old + 0.1 * scaled
    second = 0.95 * v_old + 0.05 * scaled * scaled
    master_new = master - 0.01 * (moment / (jnp.sqrt(second) + 1e-08) + 0.1 * master)
    moment_blocks = moment.reshape(blocks, -1)
    second_blocks = second.reshape(blocks, -1)
    m_scale_new = jnp.max(jnp.abs(moment_blocks), axis=1) + 1e-06
    v_scale_new = jnp.max(second_blocks, axis=1) + 1e-06
    m_code_new = (moment_blocks / m_scale_new[:, None]).reshape(master.shape).astype(bf16)
    v_code_new = (second_blocks / v_scale_new[:, None]).reshape(master.shape).astype(bf16)
    return (master_new, m_code_new, v_code_new, m_scale_new, v_scale_new)


def body(tokens, cotangent, secondary, master, m_code, v_code, m_scale, v_scale):
    width, head = tokens.shape[1], cotangent.shape[1]
    rows = master.shape[0]
    gathered = lax.all_gather(secondary, INNER, axis=0, tiled=True)
    part = lax.dot_general(
        tokens, cotangent, (((0,), (0,)), ((), ())), preferred_element_type=f32
    )
    nyh, nx, nz, nyl = (lax.axis_size(a) for a in ("yh", "x", "z", "yl"))
    part = part.reshape(nyh, nx, nz, nyl, 2, rows, head)
    part = part.transpose(4, 1, 3, 0, 2, 5, 6).reshape(2, nx * nyl, nyh * nz * rows, head)
    part = lax.optimization_barrier(part.astype(bf16))
    mine = lax.axis_index("c") == 0
    kept = jnp.where(mine, part[0], part[1])
    sent = jnp.where(mine, part[1], part[0])
    other = lax.ppermute(sent, "c", [(0, 1), (1, 0)])
    group = (kept.astype(f32) + other.astype(f32)).astype(bf16)
    group = jnp.sum(exchange(group, ("x", "yl")).astype(f32), axis=0).astype(bf16)
    group = exchange(group.reshape(nyh, nz * rows, head), "yh")
    group = jnp.sum(group.astype(f32), axis=0).astype(bf16)
    group = exchange(group.reshape(nz, rows, head), "z")
    gradient = jnp.sum(group.astype(f32), axis=0)
    total = jnp.sum(gradient * gradient)
    total = jnp.sum(to_all(jnp.broadcast_to(total, (1, head)), INNER), axis=0)
    total = jnp.sum(to_all(total, OUTER), axis=0)[0, 0]
    limit = 0.25 * math.sqrt(width * head)
    factor = limit / jnp.maximum(jnp.sqrt(total), limit)
    master_new, m_code_new, v_code_new, m_scale_new, v_scale_new = adam_update(
        gradient, factor, master, m_code, v_code, m_scale, v_scale
    )
    secondary_new = to_all(master_new.astype(bf16), OUTER).reshape(secondary.shape)
    projected = jnp.dot(tokens, gathered, preferred_element_type=f32).astype(bf16)
    return (projected, master_new, m_code_new, v_code_new, m_scale_new, v_scale_new, secondary_new)


def solution(mesh):
    split = Mesh(mesh.devices.reshape(16, 2, 2, 4, 4), OUTER_INNER)
    return jax.shard_map(
        body,
        mesh=split,
        in_specs=(
            P(OUTER_INNER, None),
            P(OUTER_INNER, None),
            P(INNER, None),
            P(INNER_OUTER, None),
            P(INNER_OUTER, None),
            P(INNER_OUTER, None),
            P(INNER_OUTER),
            P(INNER_OUTER),
        ),
        out_specs=(
            P(OUTER_INNER, None),
            P(INNER_OUTER, None),
            P(INNER_OUTER, None),
            P(INNER_OUTER, None),
            P(INNER_OUTER),
            P(INNER_OUTER),
            P(INNER, None),
        ),
        check_vma=False,
    )
```

time: 282 us -> 195 us (0.69)
  waiting for transfers between devices: 133 us -> 35.8 us
  blocking collectives: 105 us -> 74.8 us
  starting transfers between devices: 12.3 us -> 31.8 us
  local copies, waits for them, and re-layouts: 5.89 us -> 19.9 us
  other arithmetic: 3.44 us -> 10.3 us
    reduce_scatter x1 -> x0, waiting for transfers between devices: 115 us -> none  [body(): lax.psum_scatter(rounded_term(columns, cotangent).astype(jnp.bfloat16), I...]
    psum x5 -> x0, blocking collectives: 56.1 us -> none  [by_axis(): return functools.reduce(lax.psum, axes, value)]
    all_to_all x1 -> x4, blocking collectives: 49.1 us -> 74.8 us  [exchange(): return lax.all_to_all(pieces, axes, split_axis=0, concat_axis=0, tiled=True)]
    ppermute x0 -> x1, starting transfers between devices: none -> 16 us  [body(): other = lax.ppermute(sent, 'c', [(0, 1), (1, 0)])]
    all_to_all x1 -> x2, waiting for transfers between devices: 17.3 us -> 32.4 us  [exchange(): return lax.all_to_all(pieces, axes, split_axis=0, concat_axis=0, tiled=True)]
    convert_element_type x0 -> x3, local copies, waits for them, and re-layouts: none -> 13.1 us  [the longest x2 12.9 us: body(): part = lax.optimization_barrier(part.astype(bf16))]
    all_to_all x1 -> x2, starting transfers between devices: 12.2 us -> 15.8 us  [exchange(): return lax.all_to_all(pieces, axes, split_axis=0, concat_axis=0, tiled=True)]
    ppermute x0 -> x1, waiting for transfers between devices: none -> 3.33 us  [body(): other = lax.ppermute(sent, 'c', [(0, 1), (1, 0)])]
  transfers between devices with their start and end apart: 3 -> 4, of which waited for: 2 -> 3; matrix products, arithmetic and copies ran while one was open for 4% -> 6% of each run, Pallas kernels for 0% -> 0%
where the time goes in v1:
time: 195 us; the launch traced here: 194 us
  blocking collectives  74.8 us (38%)
  waiting for transfers between devices  35.8 us (18%)
  starting transfers between devices  31.8 us (16%)
  local copies, waits for them, and re-layouts  19.9 us (10%)
  between operations  14.3 us (7%)
  other arithmetic  10.3 us (5%)
  matrix products  6.94 us (4%)
    all_to_all x4, blocking collectives, exchange(): return lax.all_to_all(pieces, axes, split_axis=0, concat_axis=0, tiled=True)  74.8 us
    all_to_all x2, waiting for transfers between devices, exchange(): return lax.all_to_all(pieces, axes, split_axis=0, concat_axis=0, tiled=True)  32.4 us
    ppermute x1, starting transfers between devices, body(): other = lax.ppermute(sent, 'c', [(0, 1), (1, 0)])  16 us
    all_to_all x2, starting transfers between devices, exchange(): return lax.all_to_all(pieces, axes, split_axis=0, concat_axis=0, tiled=True)  15.8 us
    convert_element_type x2, local copies, waits for them, and re-layouts, body(): part = lax.optimization_barrier(part.astype(bf16))  12.9 us
  transfers between devices with their start and end apart: 4, of which 3 were waited for; matrix products, arithmetic and copies ran while one was open for 6% of the time, Pallas kernels for 0%

profile of v1, /device:TPU:1, one launch (start us, length us, event | category | flops | bytes accessed | tf_op | source)
XLA Modules:
  0.0 193.9 jit_solution(13172779265322927079)
XLA Ops:
  7.2 1.8 copy-done
  9.1 3.5 %convolution_convert_fusion = bf16[12288,128]{1,0:T(8,128)(2,1)} fusion(bf16[128,12288]{1,0:T(8,128)(2,1)S(1)} %copy-done, bf16[128,128]{1,0:T(8,128)(2,1)} %param.9), kind=kOutput, calls=%fused_computation | convolution fusion | flops 404226048 | bytes 6324224 | tf_op jit(solution)/shard_map/dot_general | solution.py:47
  12.5 6.2 %convert_element_type.52 = bf16[4,4,16,2,2,12,128]{6,5,4,3,2,1,0:T(8,128)(2,1)} reshape(bf16[12288,128]{1,0:T(8,128)(2,1)} %convolution_convert_fusion) | data formatting | bytes 6291456 | tf_op jit(solution)/shard_map/convert_element_type | solution.py:53
  18.7 6.8 %copy.20 = bf16[2,4,2,4,16,12,128]{6,2,1,5,4,3,0:T(2,128)(2,1)} copy(bf16[2,4,2,4,16,12,128]{6,5,0,2,4,1,3:T(8,128)(2,1)} %bitcast.19) | data formatting | bytes 6291456 | tf_op jit(solution)/shard_map/convert_element_type | solution.py:53
  25.5 3.2 %select_bitcast_fusion = bf16[8,768,128]{2,0,1:T(8,128)(2,1)} fusion(pred[]{:T(512)S(6)} %eq.3, bf16[2,8,768,128]{3,1,2,0:T(8,128)(2,1)} %bitcast.17), kind=kLoop, calls=%fused_computation.3 | loop fusion | flops 786432 | bytes 4718593 | tf_op jit(solution)/shard_map/jit(_where)/select_n | solution.py:56
  28.7 16.0 %collective-permute-start = (bf16[8,768,128]{2,0,1:T(8,128)(2,1)}, bf16[8,768,128]{2,0,1:T(8,128)(2,1)}, u32[]{:S(2)}, u32[]{:S(2)}) collective-permute-start(bf16[8,768,128]{2,0,1:T(8,128)(2,1)} %select_bitcast_fusion), channel_id=1, source_target_pairs={{0,16},{16,0},{1,17},{17,1},{2,18},{18,2},{3,19},{19,3},{4,20},{20... | collective-permute-start | bytes 4718600 | tf_op jit(solution)/shard_map/ppermute | solution.py:57
  44.7 3.3 %collective-permute-done = bf16[8,768,128]{2,0,1:T(8,128)(2,1)} collective-permute-done((bf16[8,768,128]{2,0,1:T(8,128)(2,1)}, bf16[8,768,128]{2,0,1:T(8,128)(2,1)}, u32[]{:S(2)}, u32[]{:S(2)}) %collective-permute-start) | collective-permute-done | bytes 1572896 | tf_op jit(solution)/shard_map/ppermute | solution.py:57
  48.1 3.0 %fusion = bf16[8,768,128]{2,0,1:T(8,128)(2,1)S(1)} fusion(bf16[8,768,128]{2,0,1:T(8,128)(2,1)} %collective-permute-done, pred[]{:T(512)S(6)} %eq.3, bf16[2,8,768,128]{3,1,2,0:T(8,128)(2,1)} %bitcast.18), kind=kLoop, calls=%fused_computation.2 | loop fusion | flops 3932160 | bytes 6291457 | tf_op jit(solution)/shard_map/convert_element_type | solution.py:58
  51.3 30.6 %all_to_all.30 = bf16[8,768,128]{2,1,0:T(8,128)(2,1)} all-to-all(bf16[8,768,128]{2,1,0:T(8,128)(2,1)S(1)} %copy.21), channel_id=1, replica_groups=mesh['z'=16,'yl'=2,'c'=2,'yh'=4,'x'=4] {'x','yl'}, dimensions={0} | all-to-all | bytes 3145728 | tf_op jit(solution)/shard_map/all_to_all | solution.py:17
  81.9 1.7 reduce_sum.62
  83.6 10.9 %all_to_all.31 = bf16[4,192,128]{2,1,0:T(8,128)(2,1)S(1)} all-to-all(bf16[4,192,128]{2,1,0:T(8,128)(2,1)S(1)} %bitcast.20), channel_id=1, replica_groups=mesh['z'=16,'yl'=2,'c'=2,'yh'=4,'x'=4] {'yh'}, dimensions={0} | all-to-all | bytes 393216 | tf_op jit(solution)/shard_map/all_to_all | solution.py:17
  94.6 21.1 %all_to_all.32 = bf16[16,12,128]{2,1,0:T(8,128)(2,1)S(1)} all-to-all(bf16[16,12,128]{2,1,0:T(8,128)(2,1)S(1)} %reshape.65), channel_id=1, replica_groups=mesh['z'=16,'yl'=2,'c'=2,'yh'=4,'x'=4] {'z'}, dimensions={0} | all-to-all | bytes 98304 | tf_op jit(solution)/shard_map/all_to_all | solution.py:17
  116.9 12.2 %all_to_all.33 = f32[16,1,128]{2,1,0:T(1,128)S(1)} all-to-all(f32[16,1,128]{2,1,0:T(1,128)S(1)} %broadcast_in_dim_broadcast_in_dim.3), channel_id=1, replica_groups=mesh['z'=16,'yl'=2,'c'=2,'yh'=4,'x'=4] {'yh','x'}, dimensions={0} | all-to-all | bytes 16384 | tf_op jit(solution)/shard_map/all_to_all | solution.py:17
  129.8 11.1 %all-to-all-start.4 = ((f32[64,1,128]{2,1,0:T(1,128)}), f32[64,1,128]{2,1,0:T(1,128)S(1)}, u32[]{:S(2)}, u32[]{:S(2)}) async-start(f32[64,1,128]{2,1,0:T(1,128)} %broadcast_in_dim.4), calls=%async_computation.4 | async-start | bytes 65536 | tf_op jit(solution)/shard_map/all_to_all | solution.py:17
  140.9 0.7 mul.68
  141.7 0.7 mul.78
  142.5 11.5 %all-to-all-done.4 = f32[64,1,128]{2,1,0:T(1,128)S(1)} async-done(((f32[64,1,128]{2,1,0:T(1,128)}), f32[64,1,128]{2,1,0:T(1,128)S(1)}, u32[]{:S(2)}, u32[]{:S(2)}) %all-to-all-start.4) | async-done | bytes 32800 | tf_op jit(solution)/shard_map/all_to_all | solution.py:17
  154.2 0.8 fusion.2
  155.0 0.8 broadcast_in_dim.5
  155.8 4.7 %all-to-all-start.5 = ((bf16[64,12,128]{2,1,0:T(8,128)(2,1)}), bf16[64,12,128]{2,1,0:T(8,128)(2,1)S(1)}, u32[]{:S(2)}, u32[]{:S(2)}) async-start(bf16[64,12,128]{2,1,0:T(8,128)(2,1)} %broadcast_in_dim.5), calls=%async_computation.5 | async-start | bytes 524288 | tf_op jit(solution)/shard_map/all_to_all | solution.py:17
  161.2 0.7 divide_convert_fusion
  161.9 20.9 %all-to-all-done.5 = bf16[64,12,128]{2,1,0:T(8,128)(2,1)S(1)} async-done(((bf16[64,12,128]{2,1,0:T(8,128)(2,1)}), bf16[64,12,128]{2,1,0:T(8,128)(2,1)S(1)}, u32[]{:S(2)}, u32[]{:S(2)}) %all-to-all-start.5) | async-done | bytes 196640 | tf_op jit(solution)/shard_map/all_to_all | solution.py:17
  182.8 0.7 reshape.66
  183.6 3.5 %convolution_convert_fusion.1 = bf16[128,128]{1,0:T(8,128)(2,1)} fusion(bf16[128,12288]{1,0:T(8,128)(2,1)S(1)} %copy-done, bf16[12288,128]{1,0:T(8,128)(2,1)} %all-gather.2.cloned.1.call-done), kind=kOutput, calls=%fused_computation.4 | convolution fusion | flops 402669568 | bytes 6324224 | tf_op jit(solution)/shard_map/dot_general | solution.py:73
  (34 shorter events, 3.2 us)
Async XLA Ops:
  7.2 1.9 copy-start
  7.2 176.4 %all-gather.2.cloned.1.call-start = ((), (), s32[]{:S(2)}) async-start(), calls=%async_computation.6 | async-start | bytes 3342336 | tf_op jit(solution)/shard_map/all_gather | solution.py:46
  28.7 19.4 %collective-permute-start = (bf16[8,768,128]{2,0,1:T(8,128)(2,1)}, bf16[8,768,128]{2,0,1:T(8,128)(2,1)}, u32[]{:S(2)}, u32[]{:S(2)}) collective-permute-start(bf16[8,768,128]{2,0,1:T(8,128)(2,1)} %select_bitcast_fusion), channel_id=1, source_target_pairs={{0,16},{16,0},{1,17},{17,1},{2,18},{18,2},{3,19},{19,3},{4,20},{20... | collective-permute-start | bytes 4718600 | tf_op jit(solution)/shard_map/ppermute | solution.py:57
  51.3 102.9 %copy-start.1 = (bf16[12,128]{1,0:T(8,128)(2,1)S(1)}, bf16[12,128]{1,0:T(8,128)(2,1)}, u32[]{:S(2)}) copy-start(bf16[12,128]{1,0:T(8,128)(2,1)} %param.13) | copy-start | bytes 9220
  51.3 102.9 %copy-start.2 = (bf16[12,128]{1,0:T(8,128)(2,1)S(1)}, bf16[12,128]{1,0:T(8,128)(2,1)}, u32[]{:S(2)}) copy-start(bf16[12,128]{1,0:T(8,128)(2,1)} %param.12) | copy-start | bytes 9220
  51.3 102.9 %copy-start.3 = (f32[12,128]{1,0:T(8,128)S(1)}, f32[12,128]{1,0:T(8,128)}, u32[]{:S(2)}) copy-start(f32[12,128]{1,0:T(8,128)} %param.11) | copy-start | bytes 18436
  129.8 24.2 %all-to-all-start.4 = ((f32[64,1,128]{2,1,0:T(1,128)}), f32[64,1,128]{2,1,0:T(1,128)S(1)}, u32[]{:S(2)}, u32[]{:S(2)}) async-start(f32[64,1,128]{2,1,0:T(1,128)} %broadcast_in_dim.4), calls=%async_computation.4 | async-start | bytes 65536 | tf_op jit(solution)/shard_map/all_to_all | solution.py:17
  155.8 27.1 %all-to-all-start.5 = ((bf16[64,12,128]{2,1,0:T(8,128)(2,1)}), bf16[64,12,128]{2,1,0:T(8,128)(2,1)S(1)}, u32[]{:S(2)}, u32[]{:S(2)}) async-start(bf16[64,12,128]{2,1,0:T(8,128)(2,1)} %broadcast_in_dim.5), calls=%async_computation.5 | async-start | bytes 524288 | tf_op jit(solution)/shard_map/all_to_all | solution.py:17
  160.9 26.1 %copy-start.4 = (f32[3]{0:T(128)}, f32[3]{0:T(128)S(1)}, u32[]{:S(2)}) copy-start(f32[3]{0:T(128)S(1)} %get-tuple-element.15) | copy-start | bytes 40
  160.9 26.1 %copy-start.5 = (f32[3]{0:T(128)}, f32[3]{0:T(128)S(1)}, u32[]{:S(2)}) copy-start(f32[3]{0:T(128)S(1)} %get-tuple-element.16) | copy-start | bytes 40
Sparse Core Ops, SparseCore 0:
  44.9 78.5 all-gather.1

commit v2 on v1

v2 whole, which is shorter than its diff:
```python
import functools
import math

import jax
import jax.numpy as jnp
from jax import lax
from jax.experimental import pallas as pl
from jax.experimental.pallas import tpu as pltpu
from jax.sharding import Mesh
from jax.sharding import PartitionSpec as P

INNER = ("yh", "x")
OUTER = ("zh", "zl", "yl", "c")
OUTER_INNER = OUTER + INNER
INNER_OUTER = INNER + OUTER
NZ, NYL, NC, NYH, NX = 16, 2, 2, 4, 4
SLOT = 16
bf16, f32 = jnp.bfloat16, jnp.float32
WHOLE = pl.BlockSpec(memory_space=pltpu.VMEM)
SCALARS = pl.BlockSpec(memory_space=pltpu.SMEM)


def exchange(pieces, axes):
    return lax.all_to_all(pieces, axes, split_axis=0, concat_axis=0, tiled=True)


def to_all(value, axes):
    return exchange(jnp.broadcast_to(value, (lax.axis_size(axes), *value.shape)), axes)


def swap_cores(value):
    return lax.ppermute(value, "c", [(0, 1), (1, 0)])


def gradient_kernel(
    rows, core_ref, m_scale_ref, v_scale_ref, tokens_ref, cotangent_ref, master_ref, m_code_ref,
    v_code_ref, kept_ref, sent_ref, states_ref,
):
    first = core_ref[0] == 0

    @pl.when(pl.program_id(0) == 0)
    def _():
        height = rows // m_scale_ref.shape[0]
        line = lax.broadcasted_iota(jnp.int32, master_ref.shape, 0)
        m_scale, v_scale = m_scale_ref[0], v_scale_ref[0]
        for b in range(1, m_scale_ref.shape[0]):
            m_scale = jnp.where(line < b * height, m_scale, m_scale_ref[b])
            v_scale = jnp.where(line < b * height, v_scale, v_scale_ref[b])
        master = master_ref[...]
        high = master.astype(bf16).astype(f32)
        pad = jnp.ones((SLOT - rows, master.shape[1]), f32)
        slots = (
            m_code_ref[...].astype(f32) * m_scale,
            v_code_ref[...].astype(f32) * v_scale,
            high,
            master - high,
        )
        for k, slot in enumerate(slots):
            states_ref[k * SLOT : (k + 1) * SLOT, :] = jnp.concatenate([slot, pad], axis=0).astype(bf16)

    part = lax.dot_general(
        tokens_ref[...], cotangent_ref[...], (((0,), (0,)), ((), ())), preferred_element_type=f32
    )
    chip = NC * rows
    for yl in range(NYL):
        for quad in range(NZ // 4):
            both = []
            for core in range(NC):
                starts = [
                    ((4 * quad + j) * NYL + yl) * chip + core * rows for j in range(4)
                ]
                both.append(jnp.concatenate([part[s : s + rows] for s in starts], axis=0))
            at = slice(quad * 4 * rows, (quad + 1) * 4 * rows)
            kept_ref[0, yl, 0, at, :] = jnp.where(first, both[0], both[1]).astype(bf16)
            sent_ref[0, yl, 0, at, :] = jnp.where(first, both[1], both[0]).astype(bf16)


def gradient_parts(core, tokens, cotangent, master, m_code, v_code, m_scale, v_scale):
    rows = master.shape[0]
    count, width = tokens.shape
    head = cotangent.shape[1]
    columns = width // (NYH * NX)
    shape = jax.ShapeDtypeStruct((NX, NYL, NYH, NZ * rows, head), bf16)
    spec = pl.BlockSpec((1, NYL, 1, NZ * rows, head), lambda i: (i % NX, 0, i // NX, 0, 0))
    return pl.pallas_call(
        functools.partial(gradient_kernel, rows),
        grid=(NYH * NX,),
        in_specs=[
            SCALARS,
            SCALARS,
            SCALARS,
            pl.BlockSpec((count, columns), lambda i: (0, i)),
            pl.BlockSpec((count, head), lambda i: (0, 0)),
        ]
        + [pl.BlockSpec((rows, head), lambda i: (0, 0))] * 3,
        out_specs=[spec, spec, pl.BlockSpec((4 * SLOT, head), lambda i: (0, 0))],
        out_shape=[shape, shape, jax.ShapeDtypeStruct((4 * SLOT, head), bf16)],
        name="gradient_parts",
    )(core, m_scale, v_scale, tokens, cotangent, master, m_code, v_code)


def forward_kernel(core_ref, tokens_ref, mine_ref, other_ref, out_ref, total_ref):
    step = pl.program_id(0)

    @pl.when(step == 0)
    def _():
        total_ref[...] = jnp.zeros_like(total_ref)

    half = mine_ref.shape[0]
    core = core_ref[0]
    own = tokens_ref[:, pl.ds(pl.multiple_of(core * half, half), half)]
    rest = tokens_ref[:, pl.ds(pl.multiple_of((1 - core) * half, half), half)]
    total_ref[...] += jnp.dot(own, mine_ref[...], preferred_element_type=f32) + jnp.dot(
        rest, other_ref[...], preferred_element_type=f32
    )

    @pl.when(step == pl.num_programs(0) - 1)
    def _():
        out_ref[...] = total_ref[...].astype(bf16)


def forward(core, tokens, mine, other):
    count, width = tokens.shape
    head = mine.shape[1]
    shards = NYH * NX
    half = mine.shape[0] // shards
    weight = pl.BlockSpec((half, head), lambda i: (i, 0))
    return pl.pallas_call(
        forward_kernel,
        grid=(shards,),
        in_specs=[SCALARS, pl.BlockSpec((count, width // shards), lambda i: (0, i)), weight, weight],
        out_specs=pl.BlockSpec((count, head), lambda i: (0, 0)),
        out_shape=jax.ShapeDtypeStruct((count, head), bf16),
        scratch_shapes=[pltpu.VMEM((count, head), f32)],
        name="forward",
    )(core, tokens, mine, other)


def update_kernel(
    limit, place_ref, squares_ref, sums_ref, all_sums_ref, states_ref, master_ref, m_code_ref,
    v_code_ref, m_scale_ref, v_scale_ref, master_new_ref, m_code_new_ref, v_code_new_ref,
    m_scale_new_ref, v_scale_new_ref, secondary_ref,
):
    rows, head = master_ref.shape
    blocks = m_scale_ref.shape[0]
    height = rows // blocks
    total = jnp.sum(squares_ref[...], axis=0, keepdims=True)
    factor = limit / jnp.maximum(jnp.sqrt(total), limit)
    gradient = sums_ref[pl.ds(place_ref[0] * rows, rows), :]
    for b in range(blocks):
        at = slice(b * height, (b + 1) * height)
        scaled = factor * gradient[at]
        m_old = m_code_ref[...].astype(f32)[at] * m_scale_ref[b]
        v_old = v_code_ref[...].astype(f32)[at] * v_scale_ref[b]
        moment = 0.9 * m_old + 0.1 * scaled
        second = 0.95 * v_old + 0.05 * scaled * scaled
        old = master_ref[at, :]
        master_new_ref[at, :] = old - 0.01 * (moment / (jnp.sqrt(second) + 1e-08) + 0.1 * old)
        m_top = jnp.max(jnp.abs(moment)) + 1e-06
        v_top = jnp.max(second) + 1e-06
        m_scale_new_ref[b] = m_top
        v_scale_new_ref[b] = v_top
        m_code_new_ref[at, :] = (moment / m_top).astype(bf16)
        v_code_new_ref[at, :] = (second / v_top).astype(bf16)
    pad = jnp.zeros((SLOT - rows, head), f32)
    for quad in range(NZ // 4):
        span = slice(quad * 4 * rows, (quad + 1) * 4 * rows)
        sums = [all_sums_ref[k, span, :].astype(f32) for k in range(NYL * NC)]
        new = []
        for j in range(4):
            for k in range(NYL * NC):
                scaled = factor * jnp.concatenate([sums[k][j * rows : (j + 1) * rows], pad], axis=0)
                device = (4 * quad + j) * NYL * NC + k
                m_old, v_old, high, low = (
                    states_ref[device, s * SLOT : (s + 1) * SLOT, :].astype(f32) for s in range(4)
                )
                old = high + low
                moment = 0.9 * m_old + 0.1 * scaled
                second = 0.95 * v_old + 0.05 * scaled * scaled
                value = old - 0.01 * (moment / (jnp.sqrt(second) + 1e-08) + 0.1 * old)
                new.append(value[:rows])
        out = slice(quad * 4 * NYL * NC * rows, (quad + 1) * 4 * NYL * NC * rows)
        secondary_ref[out, :] = jnp.concatenate(new, axis=0).astype(bf16)


def update(limit, place, squares, sums, all_sums, states, master, m_code, v_code, m_scale, v_scale, copy_rows):
    shape = jax.ShapeDtypeStruct
    return pl.pallas_call(
        functools.partial(update_kernel, limit),
        in_specs=[SCALARS] + [WHOLE] * 7 + [SCALARS] * 2,
        out_specs=[WHOLE] * 3 + [SCALARS] * 2 + [WHOLE],
        out_shape=[
            shape(master.shape, f32),
            shape(m_code.shape, bf16),
            shape(v_code.shape, bf16),
            shape(m_scale.shape, f32),
            shape(v_scale.shape, f32),
            shape((copy_rows, master.shape[1]), bf16),
        ],
        name="update",
    )(place, squares, sums, all_sums, states, master, m_code, v_code, m_scale, v_scale)


def body(tokens, cotangent, secondary, master, m_code, v_code, m_scale, v_scale):
    width, head = tokens.shape[1], cotangent.shape[1]
    rows, copy_rows = master.shape[0], secondary.shape[0]
    core = lax.axis_index("c")
    cores = core.reshape(1).astype(jnp.int32)
    kept, sent, own_states = gradient_parts(
        cores, tokens, cotangent, master, m_code, v_code, m_scale, v_scale
    )
    states = lax.all_gather(own_states, OUTER, axis=0, tiled=False)
    kept = kept.reshape(NX * NYL, NYH * NZ * rows, head)
    other = swap_cores(sent.reshape(kept.shape))
    group = (kept.astype(f32) + other.astype(f32)).astype(bf16)
    group = exchange(group, ("x", "yl"))
    group = jnp.sum(group.astype(f32), axis=0).astype(bf16)
    weight = lax.dynamic_slice_in_dim(secondary, core * (copy_rows // 2), copy_rows // 2, 0)
    group, weight, states = lax.optimization_barrier((group, weight, states))
    mine = lax.all_gather(weight, INNER, axis=0, tiled=True)
    group = exchange(group.reshape(NYH, NZ * rows, head), "yh")
    group = jnp.sum(group.astype(f32), axis=0).astype(bf16)
    group = jnp.sum(to_all(group, "zl").astype(f32), axis=0).astype(bf16)
    sums = jnp.sum(to_all(group, "zh").astype(f32), axis=0)
    all_sums = to_all(sums.astype(bf16), ("yl", "c"))
    all_sums, mine = lax.optimization_barrier((all_sums, mine))
    squares = jnp.sum(jnp.square(all_sums.astype(f32)))
    squares = to_all(jnp.broadcast_to(squares, (1, head)), INNER).reshape(NYH * NX, head)
    projected = forward(cores, tokens, mine, swap_cores(mine))
    squares, projected = lax.optimization_barrier((squares, projected))
    limit = 0.25 * math.sqrt(width * head)
    place = (lax.axis_index("zh") * 4 + lax.axis_index("zl")).reshape(1).astype(jnp.int32)
    results = update(
        limit, place, squares, sums, all_sums, states, master, m_code, v_code, m_scale, v_scale, copy_rows
    )
    return (projected, *results)


def solution(mesh):
    split = Mesh(mesh.devices.reshape(4, 4, 2, 2, 4, 4), OUTER_INNER)
    return jax.shard_map(
        body,
        mesh=split,
        in_specs=(
            P(OUTER_INNER, None),
            P(OUTER_INNER, None),
            P(INNER, None),
            P(INNER_OUTER, None),
            P(INNER_OUTER, None),
            P(INNER_OUTER, None),
            P(INNER_OUTER),
            P(INNER_OUTER),
        ),
        out_specs=(
            P(OUTER_INNER, None),
            P(INNER_OUTER, None),
            P(INNER_OUTER, None),
            P(INNER_OUTER, None),
            P(INNER_OUTER),
            P(INNER_OUTER),
            P(INNER, None),
        ),
        check_vma=False,
    )
```

time: 195 us -> 276 us (1.42)
  waiting for transfers between devices: 35.8 us -> 141 us
  Pallas kernels: 0 us -> 25.4 us
  blocking collectives: 74.8 us -> 58.2 us
  local copies, waits for them, and re-layouts: 19.9 us -> 3.74 us
  matrix products: 6.94 us -> 0 us
  other arithmetic: 10.3 us -> 4.04 us
  starting transfers between devices: 31.8 us -> 28.1 us
    all_gather x1 -> x2, waiting for transfers between devices: 0.01 us -> 118 us  [the longest x1 104 us: body(): states = lax.all_gather(own_states, OUTER, axis=0, tiled=False)]
    pallas_call x0 -> x3, Pallas kernels: none -> 25.4 us  [the longest x1 11.6 us: gradient_parts(): pl.pallas_call(functools.partial(gradient_kernel, rows), grid=(NYH * NX,)...]
    all_to_all x4, blocking collectives: 74.8 us -> 58.2 us  [exchange(): return lax.all_to_all(pieces, axes, split_axis=0, concat_axis=0, tiled=True)]
    convert_element_type x3 -> x0, local copies, waits for them, and re-layouts: 13.1 us -> none  [the longest x2 12.9 us: body(): part = lax.optimization_barrier(part.astype(bf16))]
    all_to_all x2, waiting for transfers between devices: 32.4 us -> 19.6 us  [exchange(): return lax.all_to_all(pieces, axes, split_axis=0, concat_axis=0, tiled=True)]
    all_to_all x2, starting transfers between devices: 15.8 us -> 8.53 us  [exchange(): return lax.all_to_all(pieces, axes, split_axis=0, concat_axis=0, tiled=True)]
    dot_general x2 -> x0, matrix products: 6.94 us -> none  [the longest x1 3.47 us: body(): jnp.dot(tokens, gathered, preferred_element_type=f32).astype(bf16)]
    ppermute x1 -> x2, starting transfers between devices: 16 us -> 19.5 us  [swap_cores(): return lax.ppermute(value, 'c', [(0, 1), (1, 0)])]
  transfers between devices with their start and end apart: 4 -> 6, of which waited for: 3 -> 4; matrix products, arithmetic and copies ran while one was open for 6% -> 1% of each run, Pallas kernels for 0% -> 4%
where the time goes in v2:
time: 276 us; the launch traced here: 275 us
  waiting for transfers between devices  141 us (51%)
  blocking collectives  58.2 us (21%)
  starting transfers between devices  28.1 us (10%)
  Pallas kernels  25.4 us (9%)
  between operations  14.2 us (5%)
  other arithmetic  4.04 us (1%)
  local copies, waits for them, and re-layouts  3.74 us (1%)
    all_gather x1, waiting for transfers between devices, body(): states = lax.all_gather(own_states, OUTER, axis=0, tiled=False)  104 us
    all_to_all x4, blocking collectives, exchange(): return lax.all_to_all(pieces, axes, split_axis=0, concat_axis=0, tiled=True)  58.2 us
    all_to_all x2, waiting for transfers between devices, exchange(): return lax.all_to_all(pieces, axes, split_axis=0, concat_axis=0, tiled=True)  19.6 us
    ppermute x2, starting transfers between devices, swap_cores(): return lax.ppermute(value, 'c', [(0, 1), (1, 0)])  19.5 us
    all_gather x1, waiting for transfers between devices, body(): mine = lax.all_gather(weight, INNER, axis=0, tiled=True)  13.5 us
    pallas_call x1, Pallas kernels, gradient_parts(): pl.pallas_call(functools.partial(gradient_kernel, rows), grid=(NYH * NX,)...  11.6 us
    pallas_call x1, Pallas kernels, forward(): pl.pallas_call(forward_kernel, grid=(shards,), in_specs=[SCALARS, pl.Bloc...  11.2 us
    all_to_all x2, starting transfers between devices, exchange(): return lax.all_to_all(pieces, axes, split_axis=0, concat_axis=0, tiled=True)  8.53 us
  transfers between devices with their start and end apart: 6, of which 4 were waited for; matrix products, arithmetic and copies ran while one was open for 1% of the time, Pallas kernels for 4%

profile of v2, /device:TPU:1, one launch (start us, length us, event | category | flops | bytes accessed | tf_op | source)
XLA Modules:
  0.0 275.1 jit_solution(12568569261089958064)
XLA Ops:
  7.2 11.6 %gradient_parts.1 = (bf16[4,2,4,192,128]{4,3,2,1,0:T(8,128)(2,1)}, bf16[4,2,4,192,128]{4,3,2,1,0:T(8,128)(2,1)}, bf16[64,128]{1,0:T(8,128)(2,1)}) custom-call(s32[1]{0:T(128)} %bitcast.core_ref, f32[3]{0:T(128)} %m_scale_ref.3, f32[3]{0:T(128)} %v_scale_ref.3, bf16[128,12288]{1,0:T(8,128)(2,1)} %tokens_ref.3, bf16[128,128]{1,0:T(8,128)(2,1)} %cotangent_ref.1, ...), custom_call_target="tpu_custom_call" | custom-call | tf_op jit(solution)/shard_map/gradient_parts/pallas_call | solution.py:85
  18.8 16.0 %collective-permute-start = (bf16[8,768,128]{2,1,0:T(8,128)(2,1)}, bf16[8,768,128]{2,1,0:T(8,128)(2,1)S(1)}, u32[]{:S(2)}, u32[]{:S(2)}) collective-permute-start(bf16[8,768,128]{2,1,0:T(8,128)(2,1)} %bitcast.12), channel_id=1, source_target_pairs={{0,16},{16,0},{1,17},{17,1},{2,18},{18,2},{3,19},{19,3},{4,20},{20... | collective-permute-start | bytes 4718600 | tf_op jit(solution)/shard_map/ppermute | solution.py:32
  34.8 3.2 %collective-permute-done = bf16[8,768,128]{2,1,0:T(8,128)(2,1)S(1)} collective-permute-done((bf16[8,768,128]{2,1,0:T(8,128)(2,1)}, bf16[8,768,128]{2,1,0:T(8,128)(2,1)S(1)}, u32[]{:S(2)}, u32[]{:S(2)}) %collective-permute-start) | collective-permute-done | bytes 1572896 | tf_op jit(solution)/shard_map/ppermute | solution.py:32
  38.0 3.0 %fusion = bf16[8,768,128]{2,1,0:T(8,128)(2,1)} fusion(bf16[8,768,128]{2,1,0:T(8,128)(2,1)} %bitcast.8, bf16[8,768,128]{2,1,0:T(8,128)(2,1)S(1)} %collective-permute-done), kind=kLoop, calls=%fused_computation.1 | loop fusion | flops 3145728 | bytes 4718592 | tf_op jit(solution)/shard_map/convert_element_type | solution.py:215
  41.0 3.6 %all-to-all-start = ((bf16[8,768,128]{2,1,0:T(8,128)(2,1)}), bf16[8,768,128]{2,1,0:T(8,128)(2,1)S(1)}, u32[]{:S(2)}, u32[]{:S(2)}) async-start(bf16[8,768,128]{2,1,0:T(8,128)(2,1)} %fusion), calls=%async_computation | async-start | bytes 3145728 | tf_op jit(solution)/shard_map/all_to_all | solution.py:24
  44.6 0.0 all-gather.6.cloned.1.call-start
  44.6 0.7 all-gather.6.cloned.1.call-update
  45.4 0.7 constant_dynamic-slice_fusion
  46.0 19.6 %all-to-all-done = bf16[8,768,128]{2,1,0:T(8,128)(2,1)S(1)} async-done(((bf16[8,768,128]{2,1,0:T(8,128)(2,1)}), bf16[8,768,128]{2,1,0:T(8,128)(2,1)S(1)}, u32[]{:S(2)}, u32[]{:S(2)}) %all-to-all-start) | async-done | bytes 1572896 | tf_op jit(solution)/shard_map/all_to_all | solution.py:24
  65.6 0.3 reduce_sum.54
  65.9 104.3 %all-gather.6.cloned.1.call-done = bf16[4096,128]{1,0:T(8,128)(2,1)} async-done(((bf16[64,128]{1,0:T(8,128)(2,1)}), bf16[4096,128]{1,0:T(8,128)(2,1)}) %all-gather.6.cloned.1.call-update) | async-done | bytes 1048592 | tf_op jit(solution)/shard_map/all_gather | solution.py:212
  170.2 14.0 %all_to_all.30 = bf16[4,192,128]{2,1,0:T(8,128)(2,1)S(1)} all-to-all(bf16[4,192,128]{2,1,0:T(8,128)(2,1)S(1)} %bitcast.10), channel_id=1, replica_groups=mesh['zh'=4,'zl'=4,'yl'=2,'c'=2,'yh'=4,'x'=4] {'yh'}, dimensions={0} | all-to-all | bytes 393216 | tf_op jit(solution)/shard_map/all_to_all | solution.py:24
  184.3 9.6 %all_to_all.31 = bf16[4,192,128]{2,1,0:T(8,128)(2,1)S(1)} all-to-all(bf16[4,192,128]{2,1,0:T(8,128)(2,1)S(1)} %broadcast_in_dim.9), channel_id=1, replica_groups=mesh['zh'=4,'zl'=4,'yl'=2,'c'=2,'yh'=4,'x'=4] {'zl'}, dimensions={0} | all-to-all | bytes 393216 | tf_op jit(solution)/shard_map/all_to_all | solution.py:24
  194.0 19.2 %all_to_all.32 = bf16[4,192,128]{2,1,0:T(8,128)(2,1)S(1)} all-to-all(bf16[4,192,128]{2,1,0:T(8,128)(2,1)S(1)} %broadcast_in_dim.10), channel_id=1, replica_groups=mesh['zh'=4,'zl'=4,'yl'=2,'c'=2,'yh'=4,'x'=4] {'zh'}, dimensions={0} | all-to-all | bytes 393216 | tf_op jit(solution)/shard_map/all_to_all | solution.py:24
  213.2 15.4 %all_to_all.33.all_sums_ref = bf16[4,192,128]{2,1,0:T(8,128)(2,1)S(1)} all-to-all(bf16[4,192,128]{2,1,0:T(8,128)(2,1)S(1)} %broadcast_in_dim.11), channel_id=1, replica_groups=mesh['zh'=4,'zl'=4,'yl'=2,'c'=2,'yh'=4,'x'=4] {'yl','c'}, dimensions={0} | all-to-all | bytes 393216 | tf_op jit(solution)/shard_map/all_to_all | solution.py:24
  228.7 13.5 %all-gather.4.cloned.1.call-done.mine_ref = bf16[6144,128]{1,0:T(8,128)(2,1)} async-done(((bf16[384,128]{1,0:T(8,128)(2,1)}), bf16[6144,128]{1,0:T(8,128)(2,1)}) %all-gather.4.cloned.1.call-update) | async-done | bytes 1572880 | tf_op jit(solution)/shard_map/all_gather | solution.py:220
  242.2 3.5 %collective-permute-start.1 = (bf16[6144,128]{1,0:T(8,128)(2,1)}, bf16[6144,128]{1,0:T(8,128)(2,1)S(1)}, u32[]{:S(2)}, u32[]{:S(2)}) collective-permute-start(bf16[6144,128]{1,0:T(8,128)(2,1)} %all-gather.4.cloned.1.call-done.mine_ref), channel_id=1, source_target_pairs={{0,16},{16,0},{1,17},{17,1},{2,18},{18,2},{3,19},{19,3},{4,20},{20... | collective-permute-start | bytes 4718600 | tf_op jit(solution)/shard_map/ppermute | solution.py:32
  245.7 0.7 multiply_reduce_fusion
  246.4 1.2 broadcast_in_dim_broadcast_in_dim.3
  247.7 5.0 %all-to-all-start.5 = ((f32[16,1,128]{2,1,0:T(1,128)}), f32[16,1,128]{2,1,0:T(1,128)S(1)}, u32[]{:S(2)}, u32[]{:S(2)}) async-start(f32[16,1,128]{2,1,0:T(1,128)} %broadcast_in_dim_broadcast_in_dim.3), calls=%async_computation.5 | async-start | bytes 16384 | tf_op jit(solution)/shard_map/all_to_all | solution.py:24
  252.7 1.1 copy-done.2
  253.8 11.2 %forward.1 = bf16[128,128]{1,0:T(8,128)(2,1)} custom-call(s32[1]{0:T(128)} %bitcast.core_ref, bf16[128,12288]{1,0:T(8,128)(2,1)} %tokens_ref.3, bf16[6144,128]{1,0:T(8,128)(2,1)} %all-gather.4.cloned.1.call-done.mine_ref, bf16[6144,128]{1,0:T(8,128)(2,1)} %copy-done.2), custom_call_target="tpu_custom_call" | custom-call | tf_op jit(solution)/shard_map/forward/pallas_call | solution.py:128
  265.0 0.6 copy-done.4
  265.6 2.6 update.1
  (19 shorter events, 0.3 us)
Async XLA Ops:
  7.2 38.2 %copy-start = (bf16[768,128]{1,0:T(8,128)(2,1)S(1)}, bf16[768,128]{1,0:T(8,128)(2,1)}, u32[]{:S(2)}) copy-start(bf16[768,128]{1,0:T(8,128)(2,1)} %param.10) | copy-start | bytes 589828
  18.8 19.3 %collective-permute-start = (bf16[8,768,128]{2,1,0:T(8,128)(2,1)}, bf16[8,768,128]{2,1,0:T(8,128)(2,1)S(1)}, u32[]{:S(2)}, u32[]{:S(2)}) collective-permute-start(bf16[8,768,128]{2,1,0:T(8,128)(2,1)} %bitcast.12), channel_id=1, source_target_pairs={{0,16},{16,0},{1,17},{17,1},{2,18},{18,2},{3,19},{19,3},{4,20},{20... | collective-permute-start | bytes 4718600 | tf_op jit(solution)/shard_map/ppermute | solution.py:32
  41.0 24.6 %all-to-all-start = ((bf16[8,768,128]{2,1,0:T(8,128)(2,1)}), bf16[8,768,128]{2,1,0:T(8,128)(2,1)S(1)}, u32[]{:S(2)}, u32[]{:S(2)}) async-start(bf16[8,768,128]{2,1,0:T(8,128)(2,1)} %fusion), calls=%async_computation | async-start | bytes 3145728 | tf_op jit(solution)/shard_map/all_to_all | solution.py:24
  44.6 125.6 %all-gather.6.cloned.1.call-start = ((), (), s32[]{:S(2)}) async-start(), calls=%async_computation.7 | async-start | bytes 1064960 | tf_op jit(solution)/shard_map/all_gather | solution.py:212
  45.3 196.9 %all-gather.4.cloned.1.call-start = ((), (), s32[]{:S(2)}) async-start(), calls=%async_computation.6 | async-start | bytes 1671168 | tf_op jit(solution)/shard_map/all_gather | solution.py:220
  213.2 51.8 %copy-start.3 = (f32[192,128]{1,0:T(8,128)}, f32[192,128]{1,0:T(8,128)S(1)}, u32[]{:S(2)}) copy-start(f32[192,128]{1,0:T(8,128)S(1)} %convert_reduce_fusion.sums_ref) | copy-start | bytes 294916
  228.7 36.3 %copy-start.1 = (bf16[4,192,128]{2,1,0:T(8,128)(2,1)}, bf16[4,192,128]{2,1,0:T(8,128)(2,1)S(1)}, u32[]{:S(2)}) copy-start(bf16[4,192,128]{2,1,0:T(8,128)(2,1)S(1)} %all_to_all.33.all_sums_ref) | copy-start | bytes 589828
  242.2 10.4 %collective-permute-start.1 = (bf16[6144,128]{1,0:T(8,128)(2,1)}, bf16[6144,128]{1,0:T(8,128)(2,1)S(1)}, u32[]{:S(2)}, u32[]{:S(2)}) collective-permute-start(bf16[6144,128]{1,0:T(8,128)(2,1)} %all-gather.4.cloned.1.call-done.mine_ref), channel_id=1, source_target_pairs={{0,16},{16,0},{1,17},{17,1},{2,18},{18,2},{3,19},{19,3},{4,20},{20... | collective-permute-start | bytes 4718600 | tf_op jit(solution)/shard_map/ppermute | solution.py:32
  247.7 17.3 %all-to-all-start.5 = ((f32[16,1,128]{2,1,0:T(1,128)}), f32[16,1,128]{2,1,0:T(1,128)S(1)}, u32[]{:S(2)}, u32[]{:S(2)}) async-start(f32[16,1,128]{2,1,0:T(1,128)} %broadcast_in_dim_broadcast_in_dim.3), calls=%async_computation.5 | async-start | bytes 16384 | tf_op jit(solution)/shard_map/all_to_all | solution.py:24
  252.6 1.2 copy-start.2
  265.0 0.6 copy-start.4
Sparse Core Ops, SparseCore 0:
  48.7 121.4 all-gather.5
  174.9 67.2 all-gather.3
